TPU v7x, 32 devices: a whole 2x2x4 slice. The times are simulated.
32 devices in a mesh: pages: 16 (over z, x, core), tok: 2 (over y).
Axes of the slice: x: 2, y: 2, z: 4, core: 2. Of those that a mesh axis runs over, the one named last changes fastest.
Arguments:
- queries: bfloat16 [32, 32, 128], P('pages'), may hold values from -50 to 50
- pages: bfloat16 [16, 1024, 128], P('pages', 'tok'), may hold values from -10 to 10
- pad_counts: int32 [16], P('pages'), may hold values from 0 to 511
- labels: int32 [32, 16], P(None, 'pages'), may hold values 0 or 1
Outputs:
- query_grad: float32 [32, 32, 128], P('pages')
- page_grad: float32 [16, 1024, 128], P('pages', 'tok')
- page_loss: float32 [16], P('pages')
All inputs are finite; a program needn't handle non-finite values. No bound on the sum of `labels` on one device may be relied on, other than what follows from the above.
Results may differ from a plain program's by a relative error of at most 0.0025.
Values may be sent and summed in bfloat16 or wider, within the bound.
No kernel may reach another device: no remote copies, remote signals or barrier semaphores. Data moves between devices by JAX's collectives and lax.ppermute only.
A program may use at most 64 MiB of HBM per device.

v0:
```python
import math
import jax
import jax.numpy as jnp
from jax import lax
from jax.sharding import PartitionSpec as P

LP = 1024
MASKED = -1000000000.0
LOGIT_SPAN = 8.0
CENTRE_SHIFT = 0.5
FILL_SHARE = 0.75


def combined_all(value, axis, combine):
    everything = lax.all_gather(value, axis)
    first = everything[0]

    def lap(k, so_far):
        return combine(so_far, everything[k])

    return lax.fori_loop(1, lax.axis_size(axis), lap, first)


def combine_smooth(former, latter):
    highest = jnp.maximum(former, latter)
    return highest + jnp.log(jnp.exp(former - highest) + jnp.exp(latter - highest))


def on_device(queries, pages, pad_counts, labels):
    query_count, query_len, feature_width = queries.shape
    local_pages, local_tokens, _ = pages.shape
    score_scale = feature_width ** (-0.5)
    token_offset = lax.axis_index("tok") * local_tokens
    positions = token_offset + jnp.arange(local_tokens, dtype=jnp.int32)
    usable = positions[None, :] < (LP - pad_counts)[:, None]
    gathered = lax.all_gather(queries, "pages", axis=0, tiled=True)
    query_total = gathered.shape[0]
    row_count = query_total * query_len
    query_rows = gathered.reshape(row_count, feature_width)
    block_rows = math.gcd(row_count, 512)
    block_count = row_count // block_rows

    def scores_for(query_block, page_no):
        raw = (
            lax.dot_general(
                query_block,
                pages[page_no],
                (((1,), (1,)), ((), ())),
                preferred_element_type=jnp.float32,
            )
            * score_scale
        )
        return jnp.where(usable[page_no][None, :], raw, MASKED)

    def forward_block(block_index, running):
        offset = block_index * block_rows
        query_block = lax.dynamic_slice_in_dim(query_rows, offset, block_rows, 0)
        scores = scores_for(query_block, 0)
        highest = jnp.max(scores, axis=1)
        columns = [highest + jnp.log(jnp.sum(jnp.exp(scores - highest[:, None]), axis=1))]
        partial_value = jnp.stack(columns, axis=1)
        return lax.dynamic_update_slice_in_dim(running, partial_value, offset, 0)

    buffered = lax.fori_loop(
        0, block_count, forward_block, jnp.zeros((row_count, local_pages), jnp.float32)
    )
    smooth = combined_all(buffered, "tok", combine_smooth)
    similarity = smooth.reshape(query_total, query_len, local_pages).sum(axis=1)
    label_sign = 2.0 * labels.astype(jnp.float32) - 1.0
    logit_gain = LOGIT_SPAN / query_len
    centre = query_len * (CENTRE_SHIFT + math.log(FILL_SHARE * LP))
    logits = logit_gain * (similarity - centre)
    page_loss = jnp.sum(jax.nn.softplus(-label_sign * logits), axis=0)
    slope = logit_gain * (-label_sign * jax.nn.sigmoid(-label_sign * logits))
    row_slope = jnp.repeat(slope, query_len, axis=0)

    def backward_block(block_index, running):
        query_terms, page_terms = running
        offset = block_index * block_rows
        query_block = lax.dynamic_slice_in_dim(query_rows, offset, block_rows, 0)
        smooth_block = lax.dynamic_slice_in_dim(smooth, offset, block_rows, 0)
        slope_block = lax.dynamic_slice_in_dim(row_slope, offset, block_rows, 0)
        scores = scores_for(query_block, 0)
        weights = jnp.where(usable[0][None, :], jnp.exp(scores - smooth_block[:, 0][:, None]), 0.0)
        scaled = (weights * slope_block[:, 0][:, None]).astype(jnp.bfloat16)
        summed = jnp.dot(scaled, pages[0], preferred_element_type=jnp.float32)
        gradients = [
            lax.dot_general(
                scaled, query_block, (((0,), (0,)), ((), ())), preferred_element_type=jnp.float32
            )
        ]
        page_terms = page_terms + jnp.stack(gradients, axis=0)
        query_terms = lax.dynamic_update_slice_in_dim(query_terms, summed * score_scale, offset, 0)
        return (query_terms, page_terms)

    start_terms = (
        jnp.zeros((row_count, feature_width), jnp.float32),
        jnp.zeros((local_pages, local_tokens, feature_width), jnp.float32),
    )
    query_terms, page_terms = lax.fori_loop(0, block_count, backward_block, start_terms)
    page_grad = page_terms * score_scale
    owned = lax.psum_scatter(query_terms, "pages", scatter_dimension=0, tiled=True)
    owned = lax.psum(owned, "tok")
    query_grad = owned.reshape(query_count, query_len, feature_width)
    return (query_grad, page_grad, page_loss)


def solution(mesh):
    return jax.shard_map(
        on_device,
        mesh=mesh,
        in_specs=(P("pages", None, None), P("pages", "tok", None), P("pages"), P(None, "pages")),
        out_specs=(P("pages", None, None), P("pages", "tok", None), P("pages")),
        check_vma=False,
    )
```

profile of v0, /device:TPU:0, one launch (start us, length us, event | category | flops | bytes accessed | tf_op | source)
XLA Modules:
  0.0 112.6 jit_solution(9280587860546555923)
XLA Ops:
  7.9 24.2 %all_gather.9 = bf16[32,32,128]{2,1,0:T(8,128)(2,1)S(1)} all-gather(bf16[2,32,128]{2,1,0:T(8,128)(2,1)} %param.8), channel_id=1, replica_groups=mesh['pages'=16,'tok'=2] {'pages'}, dimensions={0}, use_global_device_ids=true | all-gather | bytes 278528 | tf_op jit(solution)/shard_map/all_gather | solution.py:36
  32.1 1.2 %while.35 = (s32[]{:T(128)}, f32[1024,1]{0,1:T(1,128)S(1)}, bf16[1024,128]{1,0:T(8,128)(2,1)S(1)}, bf16[1,512,128]{2,1,0:T(8,128)(2,1)S(1)}, s32[]{:T(128)}, /*i...) while((s32[]{:T(128)}, f32[1024,1]{0,1:T(1,128)S(1)}, ...), condition=%wide.region_3.4_spmd.clone, body=%wide.region_0.3_spmd.clone.sunk | while | flops 68420104 | bytes 2376867 | solution.py:64
  32.1 0.3 fusion.38
  32.4 0.2 exponential_reduce_fusion.2
  32.7 0.3 fusion.38
  33.0 0.2 exponential_reduce_fusion.2
  33.2 4.4 %all-gather = f32[2048,1]{0,1:T(1,128)S(1)} all-gather(f32[1024,1]{0,1:T(1,128)S(1)} %get-tuple-element.249), channel_id=2, replica_groups=mesh['pages'=16,'tok'=2] {'tok'}, dimensions={0}, use_global_device_ids=true | all-gather | bytes 12288 | tf_op jit(solution)/shard_map/all_gather | solution.py:15
  37.6 0.1 squeeze.28
  37.8 0.1 add_reduce_fusion
  37.9 0.5 copy-done.2
  38.4 0.6 fusion.24
  39.1 0.1 broadcast_in_dim.84
  39.2 0.1 broadcast_in_dim.85
  39.3 2.4 %while.36 = (s32[]{:T(128)}, f32[1024,128]{1,0:T(8,128)S(1)}, f32[1,512,128]{2,1,0:T(8,128)S(1)}, bf16[1024,128]{1,0:T(8,128)(2,1)S(1)}, bf16[1,512,128]{2,1,0:T...) while((s32[]{:T(128)}, f32[1024,128]{1,0:T(8,128)S(1)}, ...), condition=%wide.region_6.7_spmd.clone, body=%wide.region_5.6_spmd.clone.sunk | while | flops 203097088 | bytes 2897109 | solution.py:100
  39.4 0.4 fusion.45
  39.8 0.4 fusion.47
  40.2 0.3 fusion.46
  40.5 0.4 fusion.45
  41.0 0.4 fusion.47
  41.4 0.3 fusion.46
  41.7 0.8 copy-done.1
  42.5 0.7 broadcast_multiply_fusion
  43.2 52.9 %reduce-scatter.2.cloned.1.call-done = f32[64,128]{1,0:T(8,128)} async-done(((f32[1024,128]{1,0:T(8,128)}), f32[64,128]{1,0:T(8,128)}) %reduce-scatter.2.cloned.1.call-update) | async-done | bytes 32784 | tf_op jit(solution)/shard_map/reduce_scatter | solution.py:102
  96.2 9.6 %psum.7 = f32[2,32,128]{2,1,0:T(8,128)} all-reduce(f32[2,32,128]{2,1,0:T(8,128)} %bitcast.50), channel_id=1, replica_groups=mesh['pages'=16,'tok'=2] {'tok'}, use_global_device_ids=true, to_apply=%region_8.9 | all-reduce | flops 8192 | bytes 65536 | tf_op jit(solution)/shard_map/psum | solution.py:103
  (22 shorter events, 0.4 us)
Async XLA Ops:
  7.2 89.0 %reduce-scatter.2.cloned.1.call-start = ((), (), s32[]{:S(2)}) async-start(), calls=%async_computation.1 | async-start | bytes 557056 | tf_op jit(solution)/shard_map/reduce_scatter | solution.py:102
  7.9 24.2 %copy-start = (bf16[1,512,128]{2,1,0:T(8,128)(2,1)S(1)}, bf16[1,512,128]{2,1,0:T(8,128)(2,1)}, u32[]{:S(2)}) copy-start(bf16[1,512,128]{2,1,0:T(8,128)(2,1)} %param.9) | copy-start | bytes 393220
  37.8 0.7 copy-start.2
  41.7 0.8 copy-start.1
Sparse Core Ops, SparseCore 0:
  42.6 53.4 reduce-scatter.1
where the time goes:
time: 113 us
  waiting for transfers between devices  52.9 us (47%)
  blocking collectives  38.1 us (34%)
  between operations  14.7 us (13%)
  matrix products  2.87 us (3%)
  other arithmetic  2.05 us (2%)
  local copies, waits for them, and re-layouts  1.7 us (2%)
    reduce_scatter x1, waiting for transfers between devices, on_device(): lax.psum_scatter(query_terms, 'pages', scatter_dimension=0, tiled=True)  52.9 us
    all_gather x1, blocking collectives, on_device(): gathered = lax.all_gather(queries, 'pages', axis=0, tiled=True)  24.2 us
    psum x1, blocking collectives, on_device(): owned = lax.psum(owned, 'tok')  9.55 us
    all_gather x1, blocking collectives, combined_all(): everything = lax.all_gather(value, axis)  4.36 us
  transfers between devices with their start and end apart: 1, of which 1 were waited for; matrix products, arithmetic and copies ran while one was open for 1% of the time, Pallas kernels for 0%

commit v1 on v0

--- a/solution.py
+++ b/solution.py
@@ -100,7 +100,8 @@
     query_terms, page_terms = lax.fori_loop(0, block_count, backward_block, start_terms)
     page_grad = page_terms * score_scale
     owned = lax.psum_scatter(query_terms, "pages", scatter_dimension=0, tiled=True)
-    owned = lax.psum(owned, "tok")
+    parts = lax.all_gather(owned, "tok")
+    owned = jnp.sum(parts, axis=0)
     query_grad = owned.reshape(query_count, query_len, feature_width)
     return (query_grad, page_grad, page_loss)
 

time: 113 us -> 109 us (0.965)
  blocking collectives: 38.1 us -> 33.3 us
    psum x1 -> x0, blocking collectives: 9.55 us -> none  [on_device(): owned = lax.psum(owned, 'tok')]
    all_gather x0 -> x1, blocking collectives: none -> 4.78 us  [on_device(): parts = lax.all_gather(owned, 'tok')]
where the time goes in v1:
time: 109 us; the launch traced here: 108 us
  waiting for transfers between devices  52.9 us (49%)
  blocking collectives  33.3 us (31%)
  between operations  14.7 us (13%)
  matrix products  2.89 us (3%)
  other arithmetic  2.67 us (2%)
  local copies, waits for them, and re-layouts  1.7 us (2%)
    reduce_scatter x1, waiting for transfers between devices, on_device(): lax.psum_scatter(query_terms, 'pages', scatter_dimension=0, tiled=True)  52.9 us
    all_gather x1, blocking collectives, on_device(): gathered = lax.all_gather(queries, 'pages', axis=0, tiled=True)  24.2 us
    all_gather x1, blocking collectives, on_device(): parts = lax.all_gather(owned, 'tok')  4.78 us
    all_gather x1, blocking collectives, combined_all(): everything = lax.all_gather(value, axis)  4.36 us
  transfers between devices with their start and end apart: 1, of which 1 were waited for; matrix products, arithmetic and copies ran while one was open for 1% of the time, Pallas kernels for 0%

profile of v1, /device:TPU:0, one launch (start us, length us, event | category | flops | bytes accessed | tf_op | source)
XLA Modules:
  0.0 108.4 jit_solution(3898924558347769598)
XLA Ops:
  7.9 24.2 %all_gather.15 = bf16[32,32,128]{2,1,0:T(8,128)(2,1)S(1)} all-gather(bf16[2,32,128]{2,1,0:T(8,128)(2,1)} %param.8), channel_id=1, replica_groups=mesh['pages'=16,'tok'=2] {'pages'}, dimensions={0}, use_global_device_ids=true | all-gather | bytes 278528 | tf_op jit(solution)/shard_map/all_gather | solution.py:36
  32.1 1.2 %while.35 = (s32[]{:T(128)}, f32[1024,1]{0,1:T(1,128)S(1)}, bf16[1024,128]{1,0:T(8,128)(2,1)S(1)}, bf16[1,512,128]{2,1,0:T(8,128)(2,1)S(1)}, s32[]{:T(128)}, /*i...) while((s32[]{:T(128)}, f32[1024,1]{0,1:T(1,128)S(1)}, ...), condition=%wide.region_3.4_spmd.clone, body=%wide.region_0.3_spmd.clone.sunk | while | flops 68420104 | bytes 2376867 | solution.py:64
  32.1 0.3 fusion.38
  32.4 0.2 exponential_reduce_fusion.2
  32.7 0.3 fusion.38
  33.0 0.2 exponential_reduce_fusion.2
  33.3 4.4 %all-gather = f32[2048,1]{0,1:T(1,128)S(1)} all-gather(f32[1024,1]{0,1:T(1,128)S(1)} %get-tuple-element.249), channel_id=2, replica_groups=mesh['pages'=16,'tok'=2] {'tok'}, dimensions={0}, use_global_device_ids=true | all-gather | bytes 12288 | tf_op jit(solution)/shard_map/all_gather | solution.py:15
  37.8 0.1 add_reduce_fusion
  37.9 0.5 copy-done.2
  38.5 0.6 fusion.24
  39.1 0.1 broadcast_in_dim.84
  39.2 0.1 broadcast_in_dim.85
  39.3 2.4 %while.36 = (s32[]{:T(128)}, f32[1024,128]{1,0:T(8,128)S(1)}, f32[1,512,128]{2,1,0:T(8,128)S(1)}, bf16[1024,128]{1,0:T(8,128)(2,1)S(1)}, bf16[1,512,128]{2,1,0:T...) while((s32[]{:T(128)}, f32[1024,128]{1,0:T(8,128)S(1)}, ...), condition=%wide.region_6.7_spmd.clone, body=%wide.region_5.6_spmd.clone.sunk | while | flops 203097088 | bytes 2897109 | solution.py:100
  39.4 0.4 fusion.45
  39.8 0.4 fusion.47
  40.2 0.3 fusion.46
  40.6 0.4 fusion.45
  41.0 0.4 fusion.47
  41.4 0.3 fusion.46
  41.7 0.8 copy-done.1
  42.5 0.7 broadcast_multiply_fusion
  43.2 52.9 %reduce-scatter.2.cloned.1.call-done = f32[64,128]{1,0:T(8,128)} async-done(((f32[1024,128]{1,0:T(8,128)}), f32[64,128]{1,0:T(8,128)}) %reduce-scatter.2.cloned.1.call-update) | async-done | bytes 32784 | tf_op jit(solution)/shard_map/reduce_scatter | solution.py:102
  96.1 4.8 %all-gather.1 = f32[128,128]{1,0:T(8,128)S(1)} all-gather(f32[64,128]{1,0:T(8,128)} %reduce-scatter.2.cloned.1.call-done), channel_id=3, replica_groups=mesh['pages'=16,'tok'=2] {'tok'}, dimensions={0}, use_global_device_ids=true | all-gather | bytes 98304 | tf_op jit(solution)/shard_map/all_gather | solution.py:103
  100.9 0.6 reduce_sum.43
  (23 shorter events, 0.5 us)
Async XLA Ops:
  7.2 89.0 %reduce-scatter.2.cloned.1.call-start = ((), (), s32[]{:S(2)}) async-start(), calls=%async_computation.1 | async-start | bytes 557056 | tf_op jit(solution)/shard_map/reduce_scatter | solution.py:102
  7.9 24.2 %copy-start = (bf16[1,512,128]{2,1,0:T(8,128)(2,1)S(1)}, bf16[1,512,128]{2,1,0:T(8,128)(2,1)}, u32[]{:S(2)}) copy-start(bf16[1,512,128]{2,1,0:T(8,128)(2,1)} %param.9) | copy-start | bytes 393220
  37.8 0.7 copy-start.2
  41.7 0.8 copy-start.1
Sparse Core Ops, SparseCore 0:
  42.6 53.4 reduce-scatter.1
